TPU v7x, 32 devices: a whole 2x2x4 slice. The times are simulated.
32 devices in a mesh: seq: 8 (over z, x), head: 4 (over y, core), batch: 1.
Axes of the slice: x: 2, y: 2, z: 4, core: 2. Of those that a mesh axis runs over, the one named last changes fastest.
Arguments:
- queries: bfloat16 [2048, 4096], P(('batch', 'seq', 'head')), may hold values from -6 to 6
- keys: bfloat16 [2048, 512], P(('batch', 'seq', 'head')), may hold values from -6 to 6
- values: bfloat16 [2048, 512], P(('batch', 'seq', 'head')), may hold values from -6 to 6
- page_of_block: int32 [4], P('batch'), may hold values from 0 to 2, never falling along the last dimension, each value on 1 to 2 neighbouring positions
- links: int32 [4, 4], P('batch'), may hold values 0 or 1
Outputs:
- attended: bfloat16 [2048, 4096], P(('batch', 'seq', 'head'))
Inputs may be any that keep to these rules, and one draw needn't show every extreme that they name: `page_of_block`: page numbers never fall from one block to the next.
All inputs are finite; a program needn't handle non-finite values.
Results may differ from a plain program's by a relative error of at most 0.0065.
Values may be sent and summed in bfloat16 or wider, within the bound.
No kernel may reach another device: no remote copies, remote signals or barrier semaphores. Data moves between devices by JAX's collectives and lax.ppermute only.
A program may use at most 64 MiB of HBM per device.

v0:
```python
import jax
import jax.numpy as jnp
from jax import lax
from jax.sharding import PartitionSpec as P

HEAD_SIZE = 128
BLK = 512


def local(queries, keys, values, page_of_block, links):
    query_all, key_local, value_local = (
        lax.all_to_all(queries, "head", split_axis=1, concat_axis=0, tiled=True),
        lax.all_to_all(keys, "head", split_axis=1, concat_axis=0, tiled=True),
        lax.all_to_all(values, "head", split_axis=1, concat_axis=0, tiled=True),
    )
    row_count = query_all.shape[0]
    kv_here = key_local.shape[1] // HEAD_SIZE
    group_width = query_all.shape[1] // HEAD_SIZE // kv_here
    first_row = lax.axis_index("seq") * row_count
    block_count = page_of_block.shape[0]
    block_ids = jnp.arange(block_count, dtype=jnp.int32)
    page_table = page_of_block.astype(jnp.float32)
    link_table = links.astype(jnp.float32)
    query_pos = first_row + jnp.arange(row_count, dtype=jnp.int32)
    query_onehot = (query_pos[:, None] // BLK == block_ids[None, :]).astype(jnp.float32)
    query_page = jnp.dot(query_onehot, page_table, precision=lax.Precision.HIGHEST)
    query_links = jnp.dot(query_onehot, link_table, precision=lax.Precision.HIGHEST)
    query_heads = query_all.reshape(row_count, kv_here, group_width, HEAD_SIZE)
    score_scale = HEAD_SIZE ** (-0.5)

    def block_step(running, key_block, value_block, offset):
        block_rows = key_block.shape[0]
        key_pos = offset + jnp.arange(block_rows, dtype=jnp.int32)
        key_onehot = (key_pos[:, None] // BLK == block_ids[None, :]).astype(jnp.float32)
        key_page = jnp.dot(key_onehot, page_table, precision=lax.Precision.HIGHEST)
        linked = jnp.dot(query_links, key_onehot.T, precision=lax.Precision.HIGHEST) > 0.5
        same_page = query_page[:, None] == key_page[None, :]
        allowed = jnp.where(same_page, key_pos[None, :] <= query_pos[:, None], linked)

        def attend(previous):
            maxima, totals, weighted = previous
            scores = (
                jnp.einsum(
                    "rkgd,pkd->kgrp",
                    query_heads,
                    key_block.reshape(block_rows, kv_here, HEAD_SIZE),
                    preferred_element_type=jnp.float32,
                )
                * score_scale
            )
            scores = jnp.where(allowed[None, None], scores, -1e30)
            new_max = jnp.maximum(maxima, jnp.max(scores, axis=-1))
            weights = jnp.where(allowed[None, None], jnp.exp(scores - new_max[..., None]), 0.0)
            factor = jnp.exp(maxima - new_max)
            totals = totals * factor + jnp.sum(weights, axis=-1)
            rounded = weights.astype(jnp.bfloat16)
            weighted = weighted * factor[..., None] + jnp.einsum(
                "kgrp,pkd->kgrd",
                rounded,
                value_block.reshape(block_rows, kv_here, HEAD_SIZE),
                preferred_element_type=jnp.float32,
            )
            return (new_max, totals, weighted)

        return lax.cond(jnp.any(allowed), attend, lambda previous: previous, running)

    initial = (
        jnp.full((kv_here, group_width, row_count), -1e30, jnp.float32),
        jnp.zeros((kv_here, group_width, row_count), jnp.float32),
        jnp.zeros((kv_here, group_width, row_count, HEAD_SIZE), jnp.float32),
    )
    running = initial
    key_piece = lax.all_gather(key_local, "seq", axis=0, tiled=True)
    value_piece = lax.all_gather(value_local, "seq", axis=0, tiled=True)
    piece_rows = key_piece.shape[0]
    sub_count = piece_rows // BLK
    key_split = key_piece.reshape(sub_count, BLK, key_piece.shape[1])
    value_split = value_piece.reshape(sub_count, BLK, value_piece.shape[1])

    def scan_step(state_now, scan_item):
        key_block, value_block, block_index = scan_item
        return (block_step(state_now, key_block, value_block, block_index * BLK), None)

    running, unused = lax.scan(
        scan_step, running, (key_split, value_split, jnp.arange(sub_count, dtype=jnp.int32))
    )
    maxima, totals, weighted = running
    outcome = weighted / totals[..., None]
    outcome = (
        outcome.transpose(2, 0, 1, 3)
        .reshape(row_count, kv_here * group_width * HEAD_SIZE)
        .astype(jnp.bfloat16)
    )
    return lax.all_to_all(outcome, "head", split_axis=0, concat_axis=1, tiled=True)


def solution(mesh):
    in_specs = (
        P(("batch", "seq", "head"), None),
        P(("batch", "seq", "head"), None),
        P(("batch", "seq", "head"), None),
        P("batch"),
        P("batch", None),
    )
    out_specs = P(("batch", "seq", "head"), None)
    return jax.shard_map(local, mesh=mesh, in_specs=in_specs, out_specs=out_specs, check_vma=False)
```

profile of v0, /device:TPU:0, one launch (start us, length us, event | category | flops | bytes accessed | tf_op | source)
XLA Modules:
  0.0 122.0 jit_solution(15843513809518971838)
XLA Ops:
  0.0 0.0 copy-start
  0.0 0.8 copy-done
  0.8 0.6 copy_bitcast_fusion.2
  1.5 4.3 %all-to-all-start = ((bf16[64,4,128]{2,0,1:T(8,128)(2,1)}), bf16[64,4,128]{2,0,1:T(8,128)(2,1)S(1)}, u32[]{:S(2)}, u32[]{:S(2)}) async-start(bf16[64,4,128]{2,0,1:T(8,128)(2,1)} %copy_bitcast_fusion.2), calls=%async_computation | async-start | bytes 131072 | tf_op jit(solution)/shard_map/all_to_all | solution.py:13
  5.8 1.5 %copy_bitcast_fusion.1 = bf16[64,4,128]{2,0,1:T(8,128)(2,1)} fusion(bf16[64,512]{1,0:T(8,128)(2,1)} %param.11), kind=kLoop, calls=%fused_computation.53 | loop fusion | bytes 131072 | tf_op jit(solution)/shard_map/all_to_all | solution.py:14
  7.2 0.9 fusion.41
  8.1 1.7 %all-to-all-done = bf16[64,4,128]{2,0,1:T(8,128)(2,1)S(1)} async-done(((bf16[64,4,128]{2,0,1:T(8,128)(2,1)}), bf16[64,4,128]{2,0,1:T(8,128)(2,1)S(1)}, u32[]{:S(2)}, u32[]{:S(2)}) %all-to-all-start) | async-done | bytes 65568 | tf_op jit(solution)/shard_map/all_to_all | solution.py:13
  9.9 3.3 %all-to-all-start.2 = ((bf16[64,4,128]{2,0,1:T(8,128)(2,1)}), bf16[64,4,128]{2,0,1:T(8,128)(2,1)S(1)}, u32[]{:S(2)}, u32[]{:S(2)}) async-start(bf16[64,4,128]{2,0,1:T(8,128)(2,1)} %copy_bitcast_fusion.1), calls=%async_computation.2 | async-start | bytes 131072 | tf_op jit(solution)/shard_map/all_to_all | solution.py:14
  13.2 0.8 fusion.42
  14.0 0.7 convert_element_type.31
  14.7 1.9 %copy.43 = bf16[8,4,8,1024]{3,2,0,1:T(8,128)(2,1)} copy(bf16[8,4,8,1024]{3,2,1,0:T(8,128)(2,1)} %bitcast.120) | data formatting | bytes 1048576 | tf_op jit(solution)/shard_map/all_to_all | solution.py:12
  16.6 0.6 all-to-all-done.2
  17.2 3.5 %all-to-all-start.1 = ((bf16[64,4,1024]{2,0,1:T(8,128)(2,1)}), bf16[64,4,1024]{2,0,1:T(8,128)(2,1)S(1)}, u32[]{:S(2)}, u32[]{:S(2)}) async-start(bf16[64,4,1024]{2,0,1:T(8,128)(2,1)} %bitcast.104), calls=%async_computation.1 | async-start | bytes 1048576 | tf_op jit(solution)/shard_map/all_to_all | solution.py:12
  20.7 32.4 %all_gather.6 = bf16[2048,128]{1,0:T(8,128)(2,1)S(1)} all-gather(bf16[256,128]{1,0:T(8,128)(2,1)S(1)} %bitcast.122), channel_id=1, replica_groups=mesh['seq'=8,'head'=4,'batch'=1] {'seq'}, dimensions={0}, use_global_device_ids=true | all-gather | bytes 589824 | tf_op jit(solution)/shard_map/all_gather | solution.py:73
  53.1 31.2 %all_gather.7 = bf16[2048,128]{1,0:T(8,128)(2,1)S(1)} all-gather(bf16[256,128]{1,0:T(8,128)(2,1)S(1)} %bitcast.123), channel_id=1, replica_groups=mesh['seq'=8,'head'=4,'batch'=1] {'seq'}, dimensions={0}, use_global_device_ids=true | all-gather | bytes 589824 | tf_op jit(solution)/shard_map/all_gather | solution.py:74
  84.3 0.0 all-to-all-done.1
  84.3 0.1 copy.39
  84.4 0.1 copy.31
  84.4 0.1 broadcast_in_dim.54
  84.5 23.9 %while.19 = (s32[]{:T(128)}, f32[1,8,256]{2,1,0:T(8,128)S(1)}, f32[1,8,256]{2,1,0:T(8,128)S(1)}, f32[1,8,256,128]{3,2,1,0:T(8,128)S(1)}, f32[256]{0:T(256)S(1)},...) while((s32[]{:T(128)}, f32[1,8,256]{2,1,0:T(8,128)S(1)}, ...), condition=%wide.region_6.7_spmd.clone.clone, body=%wide.region_0.6_spmd.clone.clone.sunk | while | flops 558016768 | bytes 16143707 | solution.py:84
  84.6 0.6 dynamic_slice.42
  85.8 0.3 fusion.60
  86.1 1.1 fusion.61
  87.9 3.5 %conditional.4 = ((f32[1,8,256]{2,1,0:T(8,128)S(1)}, f32[1,8,256]{2,1,0:T(8,128)S(1)}, f32[1,8,256,128]{3,2,1,0:T(8,128)S(1)})) conditional(s32[]{:T(128)} %convert_element_type.56, (f32[1,8,256]{2,1,0:T(8,128)S(1)}, f32[1,8,256]{2,1,0:T(8,128)S(1)}, f32[1,8,256,128]{3,2,1,0:T(8,128)S(1)}) %tuple.66, (pred[256,512]{0,1:T(8,128)(4,1)S(1)}, ...), branch_computations={%region_2.2_spmd, %region_3.5_spmd} | conditional | flops 551032832 | bytes 15990824 | solution.py:65
  87.9 0.8 fusion.2
  88.7 1.6 %fusion.12 = f32[1,8,256,128]{3,2,1,0:T(8,128)S(1)} fusion(f32[512,256,8]{1,0,2:T(8,128)S(1)} %get-tuple-element.409, f32[8,256]{1,0:T(8,128)S(1)} %bitcast.113, pred[256,512]{0,1:T(8,128)(4,1)S(1)} %get-tuple-element.245, f32[1,8,256,128]{3,2,1,0:T(8,128)S(1)} %get-tuple-element.250, f32[8,256]{1,0:T(8,128)S(1)} %get-tuple-element.406, ...), kind=kOutput, calls=%fused_computation.10 | convolution fusion | flops 274202624 | bytes 6569988 | tf_op jit(solution)/shard_map/while/body/eval_jaxpr/cond/branch_1_fun/kgrp,pkd->kgrd/dot_general | solution.py:57
  90.4 1.0 fusion.4
  91.4 0.6 dynamic_slice.42
  92.7 0.3 fusion.60
  93.0 1.1 fusion.61
  94.8 3.5 %conditional.4 = ((f32[1,8,256]{2,1,0:T(8,128)S(1)}, f32[1,8,256]{2,1,0:T(8,128)S(1)}, f32[1,8,256,128]{3,2,1,0:T(8,128)S(1)})) conditional(s32[]{:T(128)} %convert_element_type.56, (f32[1,8,256]{2,1,0:T(8,128)S(1)}, f32[1,8,256]{2,1,0:T(8,128)S(1)}, f32[1,8,256,128]{3,2,1,0:T(8,128)S(1)}) %tuple.66, (pred[256,512]{0,1:T(8,128)(4,1)S(1)}, ...), branch_computations={%region_2.2_spmd, %region_3.5_spmd} | conditional | flops 551032832 | bytes 15990824 | solution.py:65
  94.8 0.8 fusion.2
  95.6 1.6 %fusion.12 = f32[1,8,256,128]{3,2,1,0:T(8,128)S(1)} fusion(f32[512,256,8]{1,0,2:T(8,128)S(1)} %get-tuple-element.409, f32[8,256]{1,0:T(8,128)S(1)} %bitcast.113, pred[256,512]{0,1:T(8,128)(4,1)S(1)} %get-tuple-element.245, f32[1,8,256,128]{3,2,1,0:T(8,128)S(1)} %get-tuple-element.250, f32[8,256]{1,0:T(8,128)S(1)} %get-tuple-element.406, ...), kind=kOutput, calls=%fused_computation.10 | convolution fusion | flops 274202624 | bytes 6569988 | tf_op jit(solution)/shard_map/while/body/eval_jaxpr/cond/branch_1_fun/kgrp,pkd->kgrd/dot_general | solution.py:57
  97.2 1.0 fusion.4
  98.3 0.6 dynamic_slice.42
  99.5 0.3 fusion.60
  99.8 1.1 fusion.61
  101.7 0.6 dynamic_slice.42
  102.9 0.3 fusion.60
  103.2 1.1 fusion.61
  105.0 3.5 %conditional.4 = ((f32[1,8,256]{2,1,0:T(8,128)S(1)}, f32[1,8,256]{2,1,0:T(8,128)S(1)}, f32[1,8,256,128]{3,2,1,0:T(8,128)S(1)})) conditional(s32[]{:T(128)} %convert_element_type.56, (f32[1,8,256]{2,1,0:T(8,128)S(1)}, f32[1,8,256]{2,1,0:T(8,128)S(1)}, f32[1,8,256,128]{3,2,1,0:T(8,128)S(1)}) %tuple.66, (pred[256,512]{0,1:T(8,128)(4,1)S(1)}, ...), branch_computations={%region_2.2_spmd, %region_3.5_spmd} | conditional | flops 551032832 | bytes 15990824 | solution.py:65
  105.0 0.8 fusion.2
  105.8 1.6 %fusion.12 = f32[1,8,256,128]{3,2,1,0:T(8,128)S(1)} fusion(f32[512,256,8]{1,0,2:T(8,128)S(1)} %get-tuple-element.409, f32[8,256]{1,0:T(8,128)S(1)} %bitcast.113, pred[256,512]{0,1:T(8,128)(4,1)S(1)} %get-tuple-element.245, f32[1,8,256,128]{3,2,1,0:T(8,128)S(1)} %get-tuple-element.250, f32[8,256]{1,0:T(8,128)S(1)} %get-tuple-element.406, ...), kind=kOutput, calls=%fused_computation.10 | convolution fusion | flops 274202624 | bytes 6569988 | tf_op jit(solution)/shard_map/while/body/eval_jaxpr/cond/branch_1_fun/kgrp,pkd->kgrd/dot_general | solution.py:57
  107.4 1.0 fusion.4
  108.5 0.3 fusion.40
  108.9 0.3 copy.32
  109.2 0.2 convert_element_type.35
  109.4 11.7 %all_to_all.70 = bf16[4,64,1024]{2,1,0:T(8,128)(2,1)S(1)} all-to-all(bf16[4,64,1024]{2,1,0:T(8,128)(2,1)S(1)} %convert_element_type.35), channel_id=1, replica_groups=mesh['seq'=8,'head'=4,'batch'=1] {'head'}, dimensions={0} | all-to-all | bytes 1048576 | tf_op jit(solution)/shard_map/all_to_all | solution.py:94
  121.2 0.8 copy.38
  (22 shorter events, 0.2 us)
Async XLA Ops:
  0.0 0.8 copy-start
  1.5 8.4 %all-to-all-start = ((bf16[64,4,128]{2,0,1:T(8,128)(2,1)}), bf16[64,4,128]{2,0,1:T(8,128)(2,1)S(1)}, u32[]{:S(2)}, u32[]{:S(2)}) async-start(bf16[64,4,128]{2,0,1:T(8,128)(2,1)} %copy_bitcast_fusion.2), calls=%async_computation | async-start | bytes 131072 | tf_op jit(solution)/shard_map/all_to_all | solution.py:13
  9.9 7.4 %all-to-all-start.2 = ((bf16[64,4,128]{2,0,1:T(8,128)(2,1)}), bf16[64,4,128]{2,0,1:T(8,128)(2,1)S(1)}, u32[]{:S(2)}, u32[]{:S(2)}) async-start(bf16[64,4,128]{2,0,1:T(8,128)(2,1)} %copy_bitcast_fusion.1), calls=%async_computation.2 | async-start | bytes 131072 | tf_op jit(solution)/shard_map/all_to_all | solution.py:14
  17.2 67.0 %all-to-all-start.1 = ((bf16[64,4,1024]{2,0,1:T(8,128)(2,1)}), bf16[64,4,1024]{2,0,1:T(8,128)(2,1)S(1)}, u32[]{:S(2)}, u32[]{:S(2)}) async-start(bf16[64,4,1024]{2,0,1:T(8,128)(2,1)} %bitcast.104), calls=%async_computation.1 | async-start | bytes 1048576 | tf_op jit(solution)/shard_map/all_to_all | solution.py:12
where the time goes:
time: 123 us; the launch traced here: 122 us
  blocking collectives  75.2 us (61%)
  matrix products  14.7 us (12%)
  starting transfers between devices  11 us (9%)
  local copies, waits for them, and re-layouts  8.84 us (7%)
  loops' own time  5.51 us (4%)
  other arithmetic  4.22 us (3%)
  waiting for transfers between devices  2.38 us (2%)
    all_gather x1, blocking collectives, local(): key_piece = lax.all_gather(key_local, 'seq', axis=0, tiled=True)  32.4 us
    all_gather x1, blocking collectives, local(): value_piece = lax.all_gather(value_local, 'seq', axis=0, tiled=True)  31.2 us
    all_to_all x1, blocking collectives, local(): lax.all_to_all(outcome, 'head', split_axis=0, concat_axis=1, tiled=True)  11.7 us
    another operation x1, loops' own time, local(): lax.scan(scan_step, running, (key_split, value_split, jnp.arange(sub_coun...  5.34 us
    dot_general x3, matrix products, attend(): jnp.einsum('kgrp,pkd->kgrd', rounded, value_block.reshape(block_rows, kv_...  4.83 us
    dot_general x4, matrix products, block_step(): jnp.dot(query_links, key_onehot.T, precision=lax.Precision.HIGHEST) > 0.5  4.53 us
    all_to_all x1, starting transfers between devices, local(): lax.all_to_all(keys, 'head', split_axis=1, concat_axis=0, tiled=True)  4.26 us
    all_to_all x1, starting transfers between devices, local(): lax.all_to_all(queries, 'head', split_axis=1, concat_axis=0, tiled=True)  3.47 us
  transfers between devices with their start and end apart: 3, of which 2 were waited for; matrix products, arithmetic and copies ran while one was open for 5% of the time, Pallas kernels for 0%

commit v1 on v0

--- a/solution.py
+++ b/solution.py
@@ -7,10 +7,33 @@
 BLK = 512
 
 
+def split_up(shard, dim, peers):
+    before, after = (shard.shape[:dim], shard.shape[dim + 1 :])
+    return jnp.moveaxis(shard.reshape(*before, peers, -1, *after), dim, 0)
+
+
+def laid_out(blocks, dim):
+    blocks = jnp.moveaxis(blocks, 0, dim)
+    shape = blocks.shape
+    return blocks.reshape(*shape[:dim], shape[dim] * shape[dim + 1], *shape[dim + 2 :])
+
+
+def exchange_directly(x, axis, split_dim, concat_dim):
+    peers, index = (lax.axis_size(axis), lax.axis_index(axis))
+    tiles = split_up(x, split_dim, peers)
+    out = tiles
+    for step in range(1, peers):
+        target, source = ((index + step) % peers, (index - step) % peers)
+        sent = lax.dynamic_index_in_dim(tiles, target, 0)
+        theirs = lax.ppermute(sent, axis, [(i, (i + step) % peers) for i in range(peers)])
+        out = lax.dynamic_update_slice_in_dim(out, theirs, source, axis=0)
+    return laid_out(out, concat_dim)
+
+
 def local(queries, keys, values, page_of_block, links):
     query_all, key_local, value_local = (
         lax.all_to_all(queries, "head", split_axis=1, concat_axis=0, tiled=True),
-        lax.all_to_all(keys, "head", split_axis=1, concat_axis=0, tiled=True),
+        exchange_directly(keys, "head", 1, 0),
         lax.all_to_all(values, "head", split_axis=1, concat_axis=0, tiled=True),
     )
     row_count = query_all.shape[0]

time: 123 us -> 119 us (0.967)
  waiting for transfers between devices: 2.38 us -> 0.01 us
    ppermute x0 -> x3, starting transfers between devices: none -> 4.51 us  [exchange_directly(): lax.ppermute(sent, axis, [(i, (i + step) % peers) for i in range(peers)])]
    all_to_all x1 -> x0, starting transfers between devices: 4.26 us -> none  [local(): lax.all_to_all(keys, 'head', split_axis=1, concat_axis=0, tiled=True)]
    all_to_all x1 -> x0, waiting for transfers between devices: 1.74 us -> none  [local(): lax.all_to_all(keys, 'head', split_axis=1, concat_axis=0, tiled=True)]
  transfers between devices with their start and end apart: 3 -> 5, of which waited for: 2 -> 0; matrix products, arithmetic and copies ran while one was open for 5% -> 5% of each run, Pallas kernels for 0% -> 0%
where the time goes in v1:
time: 119 us
  blocking collectives  74.8 us (63%)
  matrix products  14.7 us (12%)
  starting transfers between devices  11.3 us (9%)
  local copies, waits for them, and re-layouts  8 us (7%)
  loops' own time  5.51 us (5%)
  other arithmetic  4.22 us (4%)
    all_gather x1, blocking collectives, local(): key_piece = lax.all_gather(key_local, 'seq', axis=0, tiled=True)  31.9 us
    all_gather x1, blocking collectives, local(): value_piece = lax.all_gather(value_local, 'seq', axis=0, tiled=True)  31.2 us
    all_to_all x1, blocking collectives, local(): lax.all_to_all(outcome, 'head', split_axis=0, concat_axis=1, tiled=True)  11.7 us
    another operation x1, loops' own time, local(): lax.scan(scan_step, running, (key_split, value_split, jnp.arange(sub_coun...  5.34 us
    dot_general x3, matrix products, attend(): jnp.einsum('kgrp,pkd->kgrd', rounded, value_block.reshape(block_rows, kv_...  4.83 us
    dot_general x4, matrix products, block_step(): jnp.dot(query_links, key_onehot.T, precision=lax.Precision.HIGHEST) > 0.5  4.53 us
    ppermute x3, starting transfers between devices, exchange_directly(): lax.ppermute(sent, axis, [(i, (i + step) % peers) for i in range(peers)])  4.51 us
    all_to_all x1, starting transfers between devices, local(): lax.all_to_all(queries, 'head', split_axis=1, concat_axis=0, tiled=True)  3.48 us
  transfers between devices with their start and end apart: 5, of which 0 were waited for; matrix products, arithmetic and copies ran while one was open for 5% of the time, Pallas kernels for 0%

profile of v1, /device:TPU:0, one launch (start us, length us, event | category | flops | bytes accessed | tf_op | source)
XLA Modules:
  0.0 118.7 jit_solution(9296855060029935273)
XLA Ops:
  0.0 0.0 copy-start
  0.0 0.9 reshape.161
  0.9 0.1 dynamic-slice_bitcast_fusion
  1.0 0.5 collective-permute-start
  1.6 2.6 %collective-permute-start.1 = (bf16[1,64,128]{2,0,1:T(2,128)(2,1)S(1)}, bf16[1,64,128]{2,0,1:T(2,128)(2,1)S(1)}, u32[]{:S(2)}, u32[]{:S(2)}) collective-permute-start(bf16[1,64,128]{2,0,1:T(2,128)(2,1)S(1)} %get-tuple-element.415), channel_id=1, source_target_pairs={{0,2},{1,3},{2,0},{3,1},{4,6},{5,7},{6,4},{7,5},{8,10},{9,11},{10,... | collective-permute-start | bytes 49160 | tf_op jit(solution)/shard_map/ppermute | solution.py:28
  4.2 1.4 %collective-permute-start.2 = (bf16[1,64,128]{2,0,1:T(2,128)(2,1)S(1)}, bf16[1,64,128]{2,0,1:T(2,128)(2,1)S(1)}, u32[]{:S(2)}, u32[]{:S(2)}) collective-permute-start(bf16[1,64,128]{2,0,1:T(2,128)(2,1)S(1)} %get-tuple-element.414), channel_id=1, source_target_pairs={{0,3},{1,0},{2,1},{3,2},{4,7},{5,4},{6,5},{7,6},{8,11},{9,8},{10,9... | collective-permute-start | bytes 49160 | tf_op jit(solution)/shard_map/ppermute | solution.py:28
  5.5 0.0 copy-done
  5.5 0.6 copy_bitcast_fusion.1
  6.2 3.3 %all-to-all-start.1 = ((bf16[64,4,128]{2,0,1:T(8,128)(2,1)}), bf16[64,4,128]{2,0,1:T(8,128)(2,1)S(1)}, u32[]{:S(2)}, u32[]{:S(2)}) async-start(bf16[64,4,128]{2,0,1:T(8,128)(2,1)} %copy_bitcast_fusion.1), calls=%async_computation.1 | async-start | bytes 131072 | tf_op jit(solution)/shard_map/all_to_all | solution.py:37
  9.5 0.9 fusion.41
  10.4 0.9 fusion.42
  11.3 0.7 convert_element_type.31
  12.0 1.9 %copy.42 = bf16[8,4,8,1024]{3,2,0,1:T(8,128)(2,1)} copy(bf16[8,4,8,1024]{3,2,1,0:T(8,128)(2,1)} %bitcast.121) | data formatting | bytes 1048576 | tf_op jit(solution)/shard_map/all_to_all | solution.py:35
  13.9 0.0 collective-permute-done
  13.9 0.1 dynamic_update_slice.9
  14.1 0.0 collective-permute-done.1
  14.1 0.2 dynamic_update_slice.10
  14.2 0.0 collective-permute-done.2
  14.2 0.2 dynamic_update_slice.11
  14.4 0.0 all-to-all-done.1
  14.4 3.5 %all-to-all-start = ((bf16[64,4,1024]{2,0,1:T(8,128)(2,1)}), bf16[64,4,1024]{2,0,1:T(8,128)(2,1)S(1)}, u32[]{:S(2)}, u32[]{:S(2)}) async-start(bf16[64,4,1024]{2,0,1:T(8,128)(2,1)} %bitcast.104), calls=%async_computation | async-start | bytes 1048576 | tf_op jit(solution)/shard_map/all_to_all | solution.py:35
  17.9 31.9 %all_gather.6 = bf16[2048,128]{1,0:T(8,128)(2,1)S(1)} all-gather(bf16[256,128]{1,0:T(8,128)(2,1)S(1)} %bitcast.124), channel_id=1, replica_groups=mesh['seq'=8,'head'=4,'batch'=1] {'seq'}, dimensions={0}, use_global_device_ids=true | all-gather | bytes 589824 | tf_op jit(solution)/shard_map/all_gather | solution.py:96
  49.8 31.2 %all_gather.7 = bf16[2048,128]{1,0:T(8,128)(2,1)S(1)} all-gather(bf16[256,128]{1,0:T(8,128)(2,1)S(1)} %bitcast.123), channel_id=1, replica_groups=mesh['seq'=8,'head'=4,'batch'=1] {'seq'}, dimensions={0}, use_global_device_ids=true | all-gather | bytes 589824 | tf_op jit(solution)/shard_map/all_gather | solution.py:97
  81.0 0.0 all-to-all-done
  81.0 0.1 copy.39
  81.1 0.1 copy.32
  81.2 0.1 broadcast_in_dim.54
  81.3 24.0 %while.19 = (s32[]{:T(128)}, f32[1,8,256]{2,1,0:T(8,128)S(1)}, f32[1,8,256]{2,1,0:T(8,128)S(1)}, f32[1,8,256,128]{3,2,1,0:T(8,128)S(1)}, f32[256]{0:T(256)S(1)},...) while((s32[]{:T(128)}, f32[1,8,256]{2,1,0:T(8,128)S(1)}, ...), condition=%wide.region_6.7_spmd.clone.clone, body=%wide.region_0.6_spmd.clone.clone.sunk | while | flops 558016768 | bytes 16143707 | solution.py:107
  81.3 0.6 dynamic_slice.55
  82.5 0.3 fusion.59
  82.8 1.1 fusion.60
  84.6 3.5 %conditional.4 = ((f32[1,8,256]{2,1,0:T(8,128)S(1)}, f32[1,8,256]{2,1,0:T(8,128)S(1)}, f32[1,8,256,128]{3,2,1,0:T(8,128)S(1)})) conditional(s32[]{:T(128)} %convert_element_type.56, (f32[1,8,256]{2,1,0:T(8,128)S(1)}, f32[1,8,256]{2,1,0:T(8,128)S(1)}, f32[1,8,256,128]{3,2,1,0:T(8,128)S(1)}) %tuple.68, (pred[256,512]{0,1:T(8,128)(4,1)S(1)}, ...), branch_computations={%region_2.2_spmd, %region_3.5_spmd} | conditional | flops 551032832 | bytes 15990824 | solution.py:88
  84.6 0.8 fusion.2
  85.4 1.6 %fusion.12 = f32[1,8,256,128]{3,2,1,0:T(8,128)S(1)} fusion(f32[512,256,8]{1,0,2:T(8,128)S(1)} %get-tuple-element.409, f32[8,256]{1,0:T(8,128)S(1)} %bitcast.113, pred[256,512]{0,1:T(8,128)(4,1)S(1)} %get-tuple-element.245, f32[1,8,256,128]{3,2,1,0:T(8,128)S(1)} %get-tuple-element.250, f32[8,256]{1,0:T(8,128)S(1)} %get-tuple-element.406, ...), kind=kOutput, calls=%fused_computation.10 | convolution fusion | flops 274202624 | bytes 6569988 | tf_op jit(solution)/shard_map/while/body/eval_jaxpr/cond/branch_1_fun/kgrp,pkd->kgrd/dot_general | solution.py:80
  87.1 1.0 fusion.4
  88.1 0.6 dynamic_slice.55
  89.4 0.3 fusion.59
  89.7 1.1 fusion.60
  91.5 3.5 %conditional.4 = ((f32[1,8,256]{2,1,0:T(8,128)S(1)}, f32[1,8,256]{2,1,0:T(8,128)S(1)}, f32[1,8,256,128]{3,2,1,0:T(8,128)S(1)})) conditional(s32[]{:T(128)} %convert_element_type.56, (f32[1,8,256]{2,1,0:T(8,128)S(1)}, f32[1,8,256]{2,1,0:T(8,128)S(1)}, f32[1,8,256,128]{3,2,1,0:T(8,128)S(1)}) %tuple.68, (pred[256,512]{0,1:T(8,128)(4,1)S(1)}, ...), branch_computations={%region_2.2_spmd, %region_3.5_spmd} | conditional | flops 551032832 | bytes 15990824 | solution.py:88
  91.5 0.8 fusion.2
  92.3 1.6 %fusion.12 = f32[1,8,256,128]{3,2,1,0:T(8,128)S(1)} fusion(f32[512,256,8]{1,0,2:T(8,128)S(1)} %get-tuple-element.409, f32[8,256]{1,0:T(8,128)S(1)} %bitcast.113, pred[256,512]{0,1:T(8,128)(4,1)S(1)} %get-tuple-element.245, f32[1,8,256,128]{3,2,1,0:T(8,128)S(1)} %get-tuple-element.250, f32[8,256]{1,0:T(8,128)S(1)} %get-tuple-element.406, ...), kind=kOutput, calls=%fused_computation.10 | convolution fusion | flops 274202624 | bytes 6569988 | tf_op jit(solution)/shard_map/while/body/eval_jaxpr/cond/branch_1_fun/kgrp,pkd->kgrd/dot_general | solution.py:80
  93.9 1.0 fusion.4
  95.0 0.6 dynamic_slice.55
  96.2 0.3 fusion.59
  96.5 1.1 fusion.60
  98.4 0.6 dynamic_slice.55
  99.6 0.3 fusion.59
  99.9 1.1 fusion.60
  101.7 3.5 %conditional.4 = ((f32[1,8,256]{2,1,0:T(8,128)S(1)}, f32[1,8,256]{2,1,0:T(8,128)S(1)}, f32[1,8,256,128]{3,2,1,0:T(8,128)S(1)})) conditional(s32[]{:T(128)} %convert_element_type.56, (f32[1,8,256]{2,1,0:T(8,128)S(1)}, f32[1,8,256]{2,1,0:T(8,128)S(1)}, f32[1,8,256,128]{3,2,1,0:T(8,128)S(1)}) %tuple.68, (pred[256,512]{0,1:T(8,128)(4,1)S(1)}, ...), branch_computations={%region_2.2_spmd, %region_3.5_spmd} | conditional | flops 551032832 | bytes 15990824 | solution.py:88
  101.7 0.8 fusion.2
  102.5 1.6 %fusion.12 = f32[1,8,256,128]{3,2,1,0:T(8,128)S(1)} fusion(f32[512,256,8]{1,0,2:T(8,128)S(1)} %get-tuple-element.409, f32[8,256]{1,0:T(8,128)S(1)} %bitcast.113, pred[256,512]{0,1:T(8,128)(4,1)S(1)} %get-tuple-element.245, f32[1,8,256,128]{3,2,1,0:T(8,128)S(1)} %get-tuple-element.250, f32[8,256]{1,0:T(8,128)S(1)} %get-tuple-element.406, ...), kind=kOutput, calls=%fused_computation.10 | convolution fusion | flops 274202624 | bytes 6569988 | tf_op jit(solution)/shard_map/while/body/eval_jaxpr/cond/branch_1_fun/kgrp,pkd->kgrd/dot_general | solution.py:80
  104.2 1.0 fusion.4
  105.2 0.3 fusion.40
  105.6 0.3 copy.33
  105.9 0.2 convert_element_type.35
  106.2 11.7 %all_to_all.51 = bf16[4,64,1024]{2,1,0:T(8,128)(2,1)S(1)} all-to-all(bf16[4,64,1024]{2,1,0:T(8,128)(2,1)S(1)} %convert_element_type.35), channel_id=1, replica_groups=mesh['seq'=8,'head'=4,'batch'=1] {'head'}, dimensions={0} | all-to-all | bytes 1048576 | tf_op jit(solution)/shard_map/all_to_all | solution.py:117
  117.9 0.8 copy.38
  (23 shorter events, 0.2 us)
Async XLA Ops:
  0.0 5.5 %copy-start = (bf16[64,512]{1,0:T(8,128)(2,1)S(1)}, bf16[64,512]{1,0:T(8,128)(2,1)}, u32[]{:S(2)}) copy-start(bf16[64,512]{1,0:T(8,128)(2,1)} %param.11) | copy-start | bytes 196612
  1.0 12.9 %collective-permute-start = (bf16[1,64,128]{2,0,1:T(2,128)(2,1)S(1)}, bf16[1,64,128]{2,0,1:T(2,128)(2,1)S(1)}, u32[]{:S(2)}, u32[]{:S(2)}) collective-permute-start(bf16[1,64,128]{2,0,1:T(2,128)(2,1)S(1)} %get-tuple-element.416), channel_id=1, source_target_pairs={{0,1},{1,2},{2,3},{3,0},{4,5},{5,6},{6,7},{7,4},{8,9},{9,10},{10,1... | collective-permute-start | bytes 49160 | tf_op jit(solution)/shard_map/ppermute | solution.py:28
  1.6 12.5 %collective-permute-start.1 = (bf16[1,64,128]{2,0,1:T(2,128)(2,1)S(1)}, bf16[1,64,128]{2,0,1:T(2,128)(2,1)S(1)}, u32[]{:S(2)}, u32[]{:S(2)}) collective-permute-start(bf16[1,64,128]{2,0,1:T(2,128)(2,1)S(1)} %get-tuple-element.415), channel_id=1, source_target_pairs={{0,2},{1,3},{2,0},{3,1},{4,6},{5,7},{6,4},{7,5},{8,10},{9,11},{10,... | collective-permute-start | bytes 49160 | tf_op jit(solution)/shard_map/ppermute | solution.py:28
  4.2 10.1 %collective-permute-start.2 = (bf16[1,64,128]{2,0,1:T(2,128)(2,1)S(1)}, bf16[1,64,128]{2,0,1:T(2,128)(2,1)S(1)}, u32[]{:S(2)}, u32[]{:S(2)}) collective-permute-start(bf16[1,64,128]{2,0,1:T(2,128)(2,1)S(1)} %get-tuple-element.414), channel_id=1, source_target_pairs={{0,3},{1,0},{2,1},{3,2},{4,7},{5,4},{6,5},{7,6},{8,11},{9,8},{10,9... | collective-permute-start | bytes 49160 | tf_op jit(solution)/shard_map/ppermute | solution.py:28
  6.2 8.2 %all-to-all-start.1 = ((bf16[64,4,128]{2,0,1:T(8,128)(2,1)}), bf16[64,4,128]{2,0,1:T(8,128)(2,1)S(1)}, u32[]{:S(2)}, u32[]{:S(2)}) async-start(bf16[64,4,128]{2,0,1:T(8,128)(2,1)} %copy_bitcast_fusion.1), calls=%async_computation.1 | async-start | bytes 131072 | tf_op jit(solution)/shard_map/all_to_all | solution.py:37
  14.4 66.6 %all-to-all-start = ((bf16[64,4,1024]{2,0,1:T(8,128)(2,1)}), bf16[64,4,1024]{2,0,1:T(8,128)(2,1)S(1)}, u32[]{:S(2)}, u32[]{:S(2)}) async-start(bf16[64,4,1024]{2,0,1:T(8,128)(2,1)} %bitcast.104), calls=%async_computation | async-start | bytes 1048576 | tf_op jit(solution)/shard_map/all_to_all | solution.py:35
